TPU v7x, 32 devices: a whole 2x2x4 slice. The times are simulated.
32 devices in a mesh: seq: 4 (over z), chan: 4 (over y, core), rep: 2 (over x).
Axes of the slice: x: 2, y: 2, z: 4, core: 2. Of those that a mesh axis runs over, the one named last changes fastest.
Arguments:
- inputs: float32 [2, 4096, 512], P('rep', 'chan', 'seq'), may hold values from -0.25 to 0.25
- out_grad: float32 [2, 4096, 512], P('rep', 'chan', 'seq'), may hold values from -6 to 6
- filters: float32 [4, 1024, 512], P('chan', 'seq'), may hold values from -0.25 to 0.25
- segment_ids: int32 [2, 512], P('rep'), may hold values from 0 to 1, as said below
Outputs:
- input_grad: float32 [2, 4096, 512], P('rep', 'chan', 'seq')
- filter_grad: float32 [4, 1024, 512], P('chan', 'seq')
Inputs may be any that keep to these rules, and one draw needn't show every extreme that they name: `segment_ids`: in each replica's row the ids are 0 up to some position and 1 from it on; that position lies between 64 and 448.
All inputs are finite; a program needn't handle non-finite values.
Results may differ from a plain program's by a relative error of at most 0.000098.
Values sent between devices are 32-bit elements; how exact they have to be, the bound alone decides.
A program may use at most 64 MiB of HBM per device.

v0:
```python
import math
import jax
import jax.numpy as jnp
from jax import lax
from jax.sharding import PartitionSpec as P


def table_pair(row_count, col_count, period):
    row_index = jnp.arange(row_count, dtype=jnp.int32)[:, None]
    col_index = jnp.arange(col_count, dtype=jnp.int32)[None, :]
    phases = row_index * col_index % period
    angles = phases.astype(jnp.float32) * (2.0 * math.pi / period)
    return (jnp.cos(angles), -jnp.sin(angles))


def contract(formula, left_part, right_part):
    return jnp.einsum(
        formula,
        left_part,
        right_part,
        precision=lax.Precision.HIGHEST,
        preferred_element_type=jnp.float32,
    )


def make_tables(length):
    full_len = 2 * length
    col_size = 128
    row_size = full_len // col_size
    half_rows = row_size // 2
    outer_cos, outer_sin = table_pair(row_size, row_size, row_size)
    fwd_cos = outer_cos[:, :half_rows]
    fwd_sin = outer_sin[:, :half_rows]
    outer_fwd = jnp.concatenate(
        [jnp.concatenate([fwd_cos, -fwd_sin], axis=1), jnp.concatenate([fwd_sin, fwd_cos], axis=1)],
        axis=0,
    )
    inv_cos = outer_cos[:half_rows]
    inv_sin = outer_sin[:half_rows]
    outer_inv = jnp.concatenate(
        [jnp.concatenate([inv_cos, inv_sin], axis=1), jnp.concatenate([-inv_sin, inv_cos], axis=1)],
        axis=0,
    )
    twiddle = table_pair(row_size, col_size, full_len)
    inner_cos, inner_sin = table_pair(col_size, col_size, col_size)
    inner_fwd = jnp.stack(
        [jnp.stack([inner_cos, inner_sin], axis=1), jnp.stack([-inner_sin, inner_cos], axis=1)],
        axis=0,
    )
    inner_inv = jnp.stack(
        [jnp.stack([inner_cos, -inner_sin], axis=1), jnp.stack([inner_sin, inner_cos], axis=1)],
        axis=0,
    )
    return (outer_fwd, outer_inv, twiddle, inner_fwd, inner_inv, half_rows, col_size)


def forward_spectrum(signal, real_only, tables):
    outer_fwd, outer_inv, twiddle, inner_fwd, inner_inv, half_rows, col_size = tables
    chan_count = signal.shape[0]
    if real_only:
        section = contract("ja,cab->cjb", outer_fwd[:, :half_rows], signal)
    else:
        section = contract(
            "ja,cab->cjb", outer_fwd, signal.reshape(chan_count, 2 * half_rows, col_size)
        )
    section = section.reshape(chan_count, 2, 2 * half_rows, col_size)
    section_re = section[:, 0]
    section_im = section[:, 1]
    turned = jnp.stack(
        [
            section_re * twiddle[0] - section_im * twiddle[1],
            section_re * twiddle[1] + section_im * twiddle[0],
        ],
        axis=1,
    )
    return contract("cpjb,pbqm->cqjm", turned, inner_fwd)


def inverse_signal(spectrum, tables, want_imag):
    outer_fwd, outer_inv, twiddle, inner_fwd, inner_inv, half_rows, col_size = tables
    chan_count = spectrum.shape[0]
    factor = 1.0 / (2 * half_rows * col_size)
    mixed = contract("cqjm,qmpb->cpjb", spectrum, inner_inv)
    mixed_re = mixed[:, 0]
    mixed_im = mixed[:, 1]
    turned = jnp.stack(
        [
            mixed_re * twiddle[0] + mixed_im * twiddle[1],
            mixed_im * twiddle[0] - mixed_re * twiddle[1],
        ],
        axis=1,
    )
    turned = turned.reshape(chan_count, 4 * half_rows, col_size)
    table = outer_inv if want_imag else outer_inv[:half_rows]
    signal = contract("aj,cjb->cab", table, turned) * factor
    return signal.reshape(chan_count, -1, half_rows, col_size)


def conj_product(left_spec, right_spec):
    left_re = left_spec[:, 0]
    left_im = left_spec[:, 1]
    right_re = right_spec[:, 0]
    right_im = right_spec[:, 1]
    return jnp.stack(
        [left_re * right_re + left_im * right_im, left_re * right_im - left_im * right_re], axis=1
    )


def pair_spectrum(whole, first_mask, second_mask, tables):
    signal = whole.reshape(-1, tables[5], tables[6])
    packed = jnp.stack([signal * first_mask, signal * second_mask], axis=1)
    return forward_spectrum(packed, False, tables)


def return_grad(filter_spec, grad_spec, first_mask, second_mask, tables, slab_width, tok_count):
    product = conj_product(filter_spec, grad_spec)
    back = inverse_signal(product, tables, True)
    grad_full = first_mask * back[:, 0] + second_mask * back[:, 1]
    chan_count = grad_full.shape[0]
    pieces = grad_full.reshape(1, chan_count, -1)
    returned = lax.all_to_all(pieces, "seq", split_axis=2, concat_axis=0, tiled=True)
    return returned.reshape(1, slab_width, tok_count)


def sum_filter_grad(act_spec, grad_spec, tables):
    product = conj_product(act_spec, grad_spec)
    signal_re = inverse_signal(product, tables, False)
    chan_count = signal_re.shape[0]
    return lax.psum(signal_re.reshape(1, chan_count, -1), "rep")


def body(inputs, out_grad, filters, segment_ids):
    seq_count = lax.axis_size("seq")
    slab_width = inputs.shape[1]
    tok_count = inputs.shape[2]
    chan_count = slab_width // seq_count
    length = tok_count * seq_count
    tables = make_tables(length)
    half_rows = tables[5]
    col_size = tables[6]
    second_mask = segment_ids[0].astype(jnp.float32).reshape(half_rows, col_size)
    first_mask = 1.0 - second_mask
    filter_spec = forward_spectrum(
        filters[0].reshape(chan_count, half_rows, col_size), True, tables
    )
    act_pieces = inputs.reshape(seq_count, chan_count, tok_count)
    grad_pieces = out_grad.reshape(seq_count, chan_count, tok_count)
    act_whole, grad_whole = (
        lax.all_to_all(act_pieces, "seq", split_axis=0, concat_axis=2, tiled=True),
        lax.all_to_all(grad_pieces, "seq", split_axis=0, concat_axis=2, tiled=True),
    )
    grad_spec = pair_spectrum(grad_whole, first_mask, second_mask, tables)
    input_grad = return_grad(
        filter_spec, grad_spec, first_mask, second_mask, tables, slab_width, tok_count
    )
    act_spec = pair_spectrum(act_whole, first_mask, second_mask, tables)
    filter_grad = sum_filter_grad(act_spec, grad_spec, tables)
    return (input_grad, filter_grad)


def solution(mesh):
    return jax.shard_map(
        body,
        mesh=mesh,
        in_specs=(
            P("rep", "chan", "seq"),
            P("rep", "chan", "seq"),
            P("chan", "seq", None),
            P("rep", None),
        ),
        out_specs=(P("rep", "chan", "seq"), P("chan", "seq", None)),
        check_vma=False,
    )
```

profile of v0, /device:TPU:0, one launch (start us, length us, event | category | flops | bytes accessed | tf_op | source)
XLA Modules:
  0.0 125.6 jit_solution(4370979219491827914)
XLA Ops:
  7.2 6.4 %all-to-all-start = ((f32[4,256,128]{2,1,0:T(8,128)}), f32[4,256,128]{2,1,0:T(8,128)S(1)}, u32[]{:S(2)}, u32[]{:S(2)}) async-start(f32[4,256,128]{2,1,0:T(8,128)} %bitcast.152), calls=%async_computation | async-start | bytes 1048576 | tf_op jit(solution)/shard_map/all_to_all | solution.py:150
  13.5 0.1 sine_negate_fusion.1
  13.6 0.1 fusion.80
  13.6 0.0 copy-start.3
  13.7 0.6 copy-done.3
  14.2 1.2 reshape_squeeze.3
  15.4 0.1 maximum_maximum_fusion
  15.5 0.3 fusion.54
  15.8 0.3 fusion.52
  16.1 0.7 fusion.44
  16.8 1.9 %convolution_bitcast_fusion = f32[256,2,8,128]{3,2,1,0:T(8,128)S(1)} fusion(f32[256,4,128]{2,1,0:T(4,128)S(1)} %reshape_squeeze.3, f32[16,8]{0,1:T(8,128)S(1)} %maximum_maximum_fusion), kind=kOutput, calls=%fused_computation.26 | convolution fusion | flops 25165824 | bytes 2623488 | tf_op jit(solution)/shard_map/ja,cab->cjb/dot_general | solution.py:17
  18.6 9.4 %all-to-all-done = f32[4,256,128]{2,1,0:T(8,128)S(1)} async-done(((f32[4,256,128]{2,1,0:T(8,128)}), f32[4,256,128]{2,1,0:T(8,128)S(1)}, u32[]{:S(2)}, u32[]{:S(2)}) %all-to-all-start) | async-done | bytes 524320 | tf_op jit(solution)/shard_map/all_to_all | solution.py:150
  28.0 4.3 %all-to-all-start.2 = ((f32[4,256,128]{2,1,0:T(8,128)}), f32[4,256,128]{2,1,0:T(8,128)}, u32[]{:S(2)}, u32[]{:S(2)}) async-start(f32[4,256,128]{2,1,0:T(8,128)} %bitcast.153), calls=%async_computation.2 | async-start | bytes 1048576 | tf_op jit(solution)/shard_map/all_to_all | solution.py:149
  32.3 0.1 sine_negate_fusion
  32.4 0.7 convert_element_type.116
  33.1 0.7 copy.73
  33.7 1.3 %copy.72 = f32[4,8]{1,0:T(4,128)} copy(f32[4,8]{0,1:T(8,128)} %bitcast.159) | data formatting | bytes 256 | tf_op jit(solution)/shard_map/slice | solution.py:38
  35.1 0.7 copy.74
  35.7 0.6 broadcast_subtract_fusion
  36.3 0.0 copy-done.1
  36.3 0.6 broadcast_subtract_fusion.1
  36.9 1.1 fusion.88
  38.1 8.2 %all-to-all-done.2 = f32[4,256,128]{2,1,0:T(8,128)} async-done(((f32[4,256,128]{2,1,0:T(8,128)}), f32[4,256,128]{2,1,0:T(8,128)}, u32[]{:S(2)}, u32[]{:S(2)}) %all-to-all-start.2) | async-done | bytes 524320 | tf_op jit(solution)/shard_map/all_to_all | solution.py:149
  46.3 1.5 %bitcast_multiply_fusion.5 = (f32[256,1,4,128]{3,0,2,1:T(8,128)S(1)}, f32[256,1,4,128]{3,0,2,1:T(8,128)S(1)}, f32[256,1,4,128]{3,0,2,1:T(8,128)S(1)}, f32[256,1,4,128]{3,0,2,1:T(8,128)S(1)}) fusion(f32[4,256,128]{2,1,0:T(8,128)} %copy-done.1, f32[4,128]{1,0:T(4,128)} %broadcast_subtract_fusion, f32[4,128]{1,0:T(4,128)S(1)} %bitcast.157, ...), kind=kLoop, calls=%fused_computation.59 | loop fusion | flops 524288 | bytes 3149824 | tf_op jit(solution)/shard_map/mul | solution.py:111
  47.7 0.2 pad_maximum_fusion.2
  47.9 0.7 copy.65
  48.6 1.9 %convolution_bitcast_fusion.2 = f32[256,2,8,128]{3,2,1,0:T(8,128)S(1)} fusion(f32[256,8,128]{2,1,0:T(8,128)S(1)} %bitcast.150, f32[16,8]{0,1:T(8,128)S(1)} %maximum_maximum_fusion), kind=kOutput, calls=%fused_computation.31 | convolution fusion | flops 50331648 | bytes 3146240 | tf_op jit(solution)/shard_map/ja,cab->cjb/dot_general | solution.py:17
  50.5 0.1 fusion.87
  50.6 0.7 copy.79
  51.3 1.9 %convolution_bitcast_fusion.1 = f32[256,2,8,128]{3,2,1,0:T(8,128)S(1)} fusion(f32[256,8,128]{2,1,0:T(8,128)S(1)} %bitcast.149, f32[16,8]{0,1:T(8,128)S(1)} %maximum_maximum_fusion), kind=kOutput, calls=%fused_computation.30 | convolution fusion | flops 50331648 | bytes 3146240 | tf_op jit(solution)/shard_map/ja,cab->cjb/dot_general | solution.py:17
  53.2 0.0 copy-start
  53.2 0.1 fusion.86
  53.3 1.1 copy-done
  54.4 1.2 multiply_subtract_fusion.2
  55.6 2.0 %fusion.21 = f32[256,2,8,128]{0,3,2,1:T(8,128)S(1)} fusion(f32[256,1,8,128]{3,0,1,2:T(8,128)S(1)} %get-tuple-element.40, f32[256,1,8,128]{3,0,1,2:T(8,128)S(1)} %get-tuple-element.41, f32[1,128,2,128]{1,3,0,2:T(8,128)S(1)} %get-tuple-element.31, f32[1,128,2,128]{1,3,0,2:T(8,128)S(1)} %get-tuple-element.34), kind=kOutput, calls=%fused_computation.29 | convolution fusion | flops 1611202560 | bytes 4456448 | tf_op jit(solution)/shard_map/cpjb,pbqm->cqjm/dot_general | solution.py:17
  57.6 2.0 %fusion.20 = f32[256,2,8,128]{0,3,2,1:T(8,128)S(1)} fusion(f32[256,1,8,128]{3,0,1,2:T(8,128)S(1)} %get-tuple-element.38, f32[256,1,8,128]{3,0,1,2:T(8,128)S(1)} %get-tuple-element.39, f32[1,128,2,128]{1,3,0,2:T(8,128)S(1)} %get-tuple-element.31, f32[1,128,2,128]{1,3,0,2:T(8,128)S(1)} %get-tuple-element.34), kind=kOutput, calls=%fused_computation.28 | convolution fusion | flops 1611202560 | bytes 4456448 | tf_op jit(solution)/shard_map/cpjb,pbqm->cqjm/dot_general | solution.py:17
  59.5 2.2 %fusion.19 = f32[256,2,8,128]{0,3,2,1:T(8,128)S(1)} fusion(f32[256,1,8,128]{3,0,1,2:T(8,128)S(1)} %get-tuple-element.9, f32[256,1,8,128]{3,0,1,2:T(8,128)S(1)} %get-tuple-element.8, f32[1,128,2,128]{1,3,0,2:T(8,128)S(1)} %get-tuple-element.31, f32[1,128,2,128]{1,3,0,2:T(8,128)S(1)} %get-tuple-element.34), kind=kOutput, calls=%fused_computation.27 | convolution fusion | flops 1611202560 | bytes 4456448 | tf_op jit(solution)/shard_map/cpjb,pbqm->cqjm/dot_general | solution.py:17
  61.7 0.0 copy-start.2
  61.7 0.5 multiply_add_fusion.1
  62.3 0.3 copy-done.2
  62.6 3.6 %fusion.22 = f32[256,2,8,128]{3,0,1,2:T(8,128)S(1)} fusion(f32[256,1,8,128]{0,3,2,1:T(8,128)S(1)} %get-tuple-element.16, f32[256,1,8,128]{0,3,2,1:T(8,128)S(1)} %get-tuple-element.17, f32[1,128,2,128]{1,3,2,0:T(8,128)S(1)} %copy-done.2, f32[1,128,2,128]{1,3,2,0:T(8,128)S(1)} %get-tuple-element.30), kind=kOutput, calls=%fused_computation.32 | convolution fusion | flops 1611202560 | bytes 4456448 | tf_op jit(solution)/shard_map/cqjm,qmpb->cpjb/dot_general | solution.py:17
  66.2 3.6 %fusion.25 = f32[256,2,8,128]{3,0,1,2:T(8,128)S(1)} fusion(f32[256,1,8,128]{0,3,2,1:T(8,128)S(1)} %get-tuple-element.3, f32[256,1,8,128]{0,3,2,1:T(8,128)S(1)} %get-tuple-element.2, f32[1,128,2,128]{1,3,2,0:T(8,128)S(1)} %copy-done.2, f32[1,128,2,128]{1,3,2,0:T(8,128)S(1)} %get-tuple-element.30), kind=kOutput, calls=%fused_computation.33 | convolution fusion | flops 1611202560 | bytes 4456448 | tf_op jit(solution)/shard_map/cqjm,qmpb->cpjb/dot_general | solution.py:17
  69.9 0.6 multiply_add_fusion
  70.5 0.0 copy-start.4
  70.5 0.2 pad_maximum_fusion
  70.7 0.5 copy-done.4
  71.2 0.0 copy-done.5
  71.2 0.0 copy-done.7
  71.2 2.4 %fusion.28 = f32[256,128,8]{1,2,0:T(8,128)S(1)} fusion(f32[256,2,8,128]{3,0,1,2:T(8,128)S(1)} %pad_maximum_fusion, f32[4,8]{1,0:T(4,128)S(1)} %copy-done.5, f32[4,8]{1,0:T(4,128)S(1)} %copy-done.7, f32[4,8]{1,0:T(4,128)S(1)} %copy-done.4), kind=kOutput, calls=%fused_computation.34 | convolution fusion | flops 50594176 | bytes 3146112 | tf_op jit(solution)/shard_map/aj,cjb->cab/dot_general | solution.py:17
  73.6 1.0 fusion.89
  74.6 0.6 copy.76
  75.2 1.5 %copy.77 = f32[256,1,4,128]{0,1,3,2:T(1,128)S(1)} copy(f32[256,1,4,128]{3,2,1,0:T(4,128)} %get-tuple-element.25) | data formatting | bytes 1048576 | tf_op jit(solution)/shard_map/slice | solution.py:118
  76.7 0.0 copy-done.6
  76.7 2.9 %fusion.37 = f32[1,256,512]{1,0,2:T(1,128)} fusion(f32[256,1,4,128]{0,1,3,2:T(1,128)S(1)} %copy.77, f32[256,1,4,128]{0,1,3,2:T(1,128)S(1)} %copy.76, f32[512]{0:T(512)S(1)} %bitcast.158, f32[512]{0:T(512)S(1)} %copy-done.6), kind=kLoop, calls=%fused_computation.56 | loop fusion | flops 393216 | bytes 1576960 | tf_op jit(solution)/shard_map/add | solution.py:118
  79.6 3.5 %all-to-all-start.1 = ((f32[1,256,512]{1,0,2:T(1,128)}), f32[1,256,512]{1,0,2:T(1,128)S(1)}, u32[]{:S(2)}, u32[]{:S(2)}) async-start(f32[1,256,512]{1,0,2:T(1,128)} %fusion.37), calls=%async_computation.1 | async-start | bytes 1048576 | tf_op jit(solution)/shard_map/all_to_all | solution.py:121
  83.0 0.0 all-reduce.2.cloned.1.call-start
  83.1 0.2 pad_maximum_fusion.1
  83.3 2.4 %fusion.34 = f32[256,4,128]{2,1,0:T(4,128)S(1)} fusion(f32[256,2,8,128]{3,0,1,2:T(8,128)S(1)} %pad_maximum_fusion.1, f32[4,8]{1,0:T(4,128)S(1)} %copy-done.4, f32[4,8]{1,0:T(4,128)S(1)} %copy-done.5), kind=kOutput, calls=%fused_computation.36 | convolution fusion | flops 25296960 | bytes 2621696 | tf_op jit(solution)/shard_map/aj,cjb->cab/dot_general | solution.py:17
  85.7 1.0 reshape_reshape.3
  86.7 0.0 all-reduce.2.cloned.1.call-update
  86.7 10.3 %all-to-all-done.1 = f32[1,256,512]{1,0,2:T(1,128)S(1)} async-done(((f32[1,256,512]{1,0,2:T(1,128)}), f32[1,256,512]{1,0,2:T(1,128)S(1)}, u32[]{:S(2)}, u32[]{:S(2)}) %all-to-all-start.1) | async-done | bytes 524320 | tf_op jit(solution)/shard_map/all_to_all | solution.py:121
  97.1 1.0 copy.78
  98.1 18.8 %all-reduce.2.cloned.1.call-done = f32[1,256,512]{2,1,0:T(8,128)} async-done(((f32[1,256,512]{2,1,0:T(8,128)}), f32[1,256,512]{2,1,0:T(8,128)}) %all-reduce.2.cloned.1.call-update) | async-done | bytes 524304 | tf_op jit(solution)/shard_map/psum | solution.py:129
  116.9 1.9 %copy.150 = f32[1,256,512]{2,1,0:T(8,128)} copy(f32[1,256,512]{2,1,0:T(8,128)} %all-reduce.2.cloned.1.call-done) | data formatting | bytes 1048576
  (8 shorter events, 0.1 us)
Async XLA Ops:
  7.2 20.8 %all-to-all-start = ((f32[4,256,128]{2,1,0:T(8,128)}), f32[4,256,128]{2,1,0:T(8,128)S(1)}, u32[]{:S(2)}, u32[]{:S(2)}) async-start(f32[4,256,128]{2,1,0:T(8,128)} %bitcast.152), calls=%async_computation | async-start | bytes 1048576 | tf_op jit(solution)/shard_map/all_to_all | solution.py:150
  13.6 0.6 copy-start.3
  28.0 8.3 %copy-start.1 = (f32[4,256,128]{2,1,0:T(8,128)}, f32[4,256,128]{2,1,0:T(8,128)S(1)}, u32[]{:S(2)}) copy-start(f32[4,256,128]{2,1,0:T(8,128)S(1)} %all-to-all-done) | copy-start | bytes 1572868
  28.0 18.3 %all-to-all-start.2 = ((f32[4,256,128]{2,1,0:T(8,128)}), f32[4,256,128]{2,1,0:T(8,128)}, u32[]{:S(2)}, u32[]{:S(2)}) async-start(f32[4,256,128]{2,1,0:T(8,128)} %bitcast.153), calls=%async_computation.2 | async-start | bytes 1048576 | tf_op jit(solution)/shard_map/all_to_all | solution.py:149
  53.2 1.2 copy-start
  61.7 0.9 copy-start.2
  70.5 0.7 copy-start.4
  70.5 0.7 copy-start.5
  70.5 0.7 copy-start.7
  73.6 3.1 %copy-start.6 = (f32[512]{0:T(512)S(1)}, f32[512]{0:T(512)}, u32[]{:S(2)}) copy-start(f32[512]{0:T(512)} %broadcast_subtract_fusion.1) | copy-start | bytes 6148
  79.6 17.5 %all-to-all-start.1 = ((f32[1,256,512]{1,0,2:T(1,128)}), f32[1,256,512]{1,0,2:T(1,128)S(1)}, u32[]{:S(2)}, u32[]{:S(2)}) async-start(f32[1,256,512]{1,0,2:T(1,128)} %fusion.37), calls=%async_computation.1 | async-start | bytes 1048576 | tf_op jit(solution)/shard_map/all_to_all | solution.py:121
  83.0 33.9 %all-reduce.2.cloned.1.call-start = ((), (), s32[]{:S(2)}) async-start(), calls=%async_computation.3 | async-start | bytes 1048576 | tf_op jit(solution)/shard_map/psum | solution.py:129
Sparse Core Ops, SparseCore 0:
  86.8 30.0 all-reduce.1
where the time goes:
time: 126 us
  waiting for transfers between devices  46.7 us (37%)
  matrix products  23.7 us (19%)
  local copies, waits for them, and re-layouts  16.1 us (13%)
  between operations  14.3 us (11%)
  starting transfers between devices  14.2 us (11%)
  other arithmetic  10.5 us (8%)
    dot_general x10, matrix products, contract(): jnp.einsum(formula, left_part, right_part, precision=lax.Precision.HIGHES...  23.7 us
    psum x1, waiting for transfers between devices, sum_filter_grad(): return lax.psum(signal_re.reshape(1, chan_count, -1), 'rep')  18.8 us
    all_to_all x1, waiting for transfers between devices, return_grad(): lax.all_to_all(pieces, 'seq', split_axis=2, concat_axis=0, tiled=True)  10.3 us
    all_to_all x1, waiting for transfers between devices, body(): lax.all_to_all(grad_pieces, 'seq', split_axis=0, concat_axis=2, tiled=True)  9.36 us
    all_to_all x1, waiting for transfers between devices, body(): lax.all_to_all(act_pieces, 'seq', split_axis=0, concat_axis=2, tiled=True)  8.21 us
    all_to_all x1, starting transfers between devices, body(): lax.all_to_all(grad_pieces, 'seq', split_axis=0, concat_axis=2, tiled=True)  6.36 us
    unnamed x18, local copies, waits for them, and re-layouts  4.41 us
    all_to_all x1, starting transfers between devices, body(): lax.all_to_all(act_pieces, 'seq', split_axis=0, concat_axis=2, tiled=True)  4.32 us
  transfers between devices with their start and end apart: 4, of which 4 were waited for; matrix products, arithmetic and copies ran while one was open for 12% of the time, Pallas kernels for 0%

commit v1 on v0

--- a/solution.py
+++ b/solution.py
@@ -3,6 +3,8 @@
 import jax.numpy as jnp
 from jax import lax
 from jax.sharding import PartitionSpec as P
+
+state_the_inputs = lambda u: jnp.sum(lax.all_gather(u, axis_name="rep"), axis=0)
 
 
 def table_pair(row_count, col_count, period):
@@ -126,7 +128,7 @@
     product = conj_product(act_spec, grad_spec)
     signal_re = inverse_signal(product, tables, False)
     chan_count = signal_re.shape[0]
-    return lax.psum(signal_re.reshape(1, chan_count, -1), "rep")
+    return state_the_inputs(signal_re.reshape(1, chan_count, -1))
 
 
 def body(inputs, out_grad, filters, segment_ids):

time: 126 us -> 108 us (0.86)
  waiting for transfers between devices: 46.7 us -> 17.5 us
  blocking collectives: 0 us -> 16.4 us
  starting transfers between devices: 14.2 us -> 10.7 us
  local copies, waits for them, and re-layouts: 16.1 us -> 13.1 us
    psum x1 -> x0, waiting for transfers between devices: 18.8 us -> none  [sum_filter_grad(): return lax.psum(signal_re.reshape(1, chan_count, -1), 'rep')]
    all_to_all x0 -> x1, blocking collectives: none -> 16.4 us  [return_grad(): lax.all_to_all(pieces, 'seq', split_axis=2, concat_axis=0, tiled=True)]
    all_to_all x1 -> x0, waiting for transfers between devices: 10.3 us -> none  [return_grad(): lax.all_to_all(pieces, 'seq', split_axis=2, concat_axis=0, tiled=True)]
    all_to_all x1 -> x0, starting transfers between devices: 3.47 us -> none  [return_grad(): lax.all_to_all(pieces, 'seq', split_axis=2, concat_axis=0, tiled=True)]
    reduce_sum x0 -> x1, other arithmetic: none -> 2.15 us  [jnp.sum(lax.all_gather(u, axis_name='rep'), axis=0)]
    slice x3, local copies, waits for them, and re-layouts: 3.07 us -> 1.39 us  [return_grad(): grad_full = first_mask * back[:, 0] + second_mask * back[:, 1]]
    unnamed x18 -> x17, local copies, waits for them, and re-layouts: 4.41 us -> 3.04 us
  transfers between devices with their start and end apart: 4 -> 3, of which waited for: 4 -> 2; matrix products, arithmetic and copies ran while one was open for 12% -> 16% of each run, Pallas kernels for 0% -> 0%
where the time goes in v1:
time: 108 us
  matrix products  23.9 us (22%)
  waiting for transfers between devices  17.5 us (16%)
  blocking collectives  16.4 us (15%)
  between operations  14.3 us (13%)
  local copies, waits for them, and re-layouts  13.1 us (12%)
  other arithmetic  11.7 us (11%)
  starting transfers between devices  10.7 us (10%)
    dot_general x10, matrix products, contract(): jnp.einsum(formula, left_part, right_part, precision=lax.Precision.HIGHES...  23.9 us
    all_to_all x1, blocking collectives, return_grad(): lax.all_to_all(pieces, 'seq', split_axis=2, concat_axis=0, tiled=True)  16.4 us
    all_to_all x1, waiting for transfers between devices, body(): lax.all_to_all(grad_pieces, 'seq', split_axis=0, concat_axis=2, tiled=True)  9.36 us
    all_to_all x1, waiting for transfers between devices, body(): lax.all_to_all(act_pieces, 'seq', split_axis=0, concat_axis=2, tiled=True)  8.15 us
    all_to_all x1, starting transfers between devices, body(): lax.all_to_all(grad_pieces, 'seq', split_axis=0, concat_axis=2, tiled=True)  6.36 us
    all_to_all x1, starting transfers between devices, body(): lax.all_to_all(act_pieces, 'seq', split_axis=0, concat_axis=2, tiled=True)  4.13 us
    unnamed x17, local copies, waits for them, and re-layouts  3.04 us
  transfers between devices with their start and end apart: 3, of which 2 were waited for; matrix products, arithmetic and copies ran while one was open for 16% of the time, Pallas kernels for 0%

profile of v1, /device:TPU:0, one launch (start us, length us, event | category | flops | bytes accessed | tf_op | source)
XLA Modules:
  0.0 107.8 jit_solution(15885615457394658844)
XLA Ops:
  7.2 6.4 %all-to-all-start = ((f32[4,256,128]{2,1,0:T(8,128)}), f32[4,256,128]{2,1,0:T(8,128)S(1)}, u32[]{:S(2)}, u32[]{:S(2)}) async-start(f32[4,256,128]{2,1,0:T(8,128)} %bitcast.153), calls=%async_computation | async-start | bytes 1048576 | tf_op jit(solution)/shard_map/all_to_all | solution.py:152
  13.5 0.1 sine_negate_fusion.1
  13.6 0.1 fusion.80
  13.6 0.0 copy-start.3
  13.7 0.6 copy-done.3
  14.2 1.2 %reshape_squeeze.3 = f32[256,4,128]{2,1,0:T(4,128)S(1)} reshape(f32[1,256,512]{2,1,0:T(8,128)} %param.6) | data formatting | bytes 1048576 | tf_op jit(solution)/shard_map/reshape;squeeze | solution.py:146
  15.4 0.1 maximum_maximum_fusion
  15.5 0.3 fusion.54
  15.8 0.3 fusion.52
  16.1 0.7 fusion.44
  16.8 1.9 %convolution_bitcast_fusion = f32[256,2,8,128]{3,2,1,0:T(8,128)S(1)} fusion(f32[256,4,128]{2,1,0:T(4,128)S(1)} %reshape_squeeze.3, f32[16,8]{0,1:T(8,128)S(1)} %maximum_maximum_fusion), kind=kOutput, calls=%fused_computation.26 | convolution fusion | flops 25165824 | bytes 2623488 | tf_op jit(solution)/shard_map/ja,cab->cjb/dot_general | solution.py:19
  18.7 9.4 %all-to-all-done = f32[4,256,128]{2,1,0:T(8,128)S(1)} async-done(((f32[4,256,128]{2,1,0:T(8,128)}), f32[4,256,128]{2,1,0:T(8,128)S(1)}, u32[]{:S(2)}, u32[]{:S(2)}) %all-to-all-start) | async-done | bytes 524320 | tf_op jit(solution)/shard_map/all_to_all | solution.py:152
  28.0 4.1 %all-to-all-start.2 = ((f32[4,256,128]{2,1,0:T(8,128)}), f32[4,256,128]{2,1,0:T(8,128)}, u32[]{:S(2)}, u32[]{:S(2)}) async-start(f32[4,256,128]{2,1,0:T(8,128)} %bitcast.154), calls=%async_computation.2 | async-start | bytes 1048576 | tf_op jit(solution)/shard_map/all_to_all | solution.py:151
  32.2 0.2 all-gather.2.cloned.1.call-start
  32.4 0.1 sine_negate_fusion
  32.4 0.7 convert_element_type.116
  33.1 0.7 copy.73
  33.8 1.3 %copy.72 = f32[4,8]{1,0:T(4,128)} copy(f32[4,8]{0,1:T(8,128)} %bitcast.161) | data formatting | bytes 256 | tf_op jit(solution)/shard_map/slice | solution.py:40
  35.1 0.7 copy.74
  35.8 0.6 broadcast_subtract_fusion
  36.4 0.0 copy-done.1
  36.4 0.6 broadcast_subtract_fusion.1
  37.0 1.2 %fusion.88 = (f32[256,1,8,128]{3,2,1,0:T(8,128)S(1)}, f32[256,1,8,128]{3,2,1,0:T(8,128)}) fusion(f32[256,2,8,128]{3,2,1,0:T(8,128)S(1)} %convolution_bitcast_fusion), kind=kLoop, calls=%fused_computation.134 | loop fusion | bytes 4194304 | tf_op jit(solution)/shard_map/slice | solution.py:69
  38.1 8.2 %all-to-all-done.2 = f32[4,256,128]{2,1,0:T(8,128)} async-done(((f32[4,256,128]{2,1,0:T(8,128)}), f32[4,256,128]{2,1,0:T(8,128)}, u32[]{:S(2)}, u32[]{:S(2)}) %all-to-all-start.2) | async-done | bytes 524320 | tf_op jit(solution)/shard_map/all_to_all | solution.py:151
  46.3 1.5 %bitcast_multiply_fusion.5 = (f32[256,1,4,128]{3,0,2,1:T(8,128)S(1)}, f32[256,1,4,128]{3,0,2,1:T(8,128)S(1)}, f32[256,1,4,128]{3,0,2,1:T(8,128)S(1)}, f32[256,1,4,128]{3,0,2,1:T(8,128)S(1)}) fusion(f32[4,256,128]{2,1,0:T(8,128)} %copy-done.1, f32[4,128]{1,0:T(4,128)} %broadcast_subtract_fusion, f32[4,128]{1,0:T(4,128)S(1)} %bitcast.159, ...), kind=kLoop, calls=%fused_computation.59 | loop fusion | flops 524288 | bytes 3149824 | tf_op jit(solution)/shard_map/mul | solution.py:113
  47.7 0.2 pad_maximum_fusion.2
  47.9 0.7 copy.65
  48.6 1.8 %convolution_bitcast_fusion.2 = f32[256,2,8,128]{3,2,1,0:T(8,128)S(1)} fusion(f32[256,8,128]{2,1,0:T(8,128)S(1)} %bitcast.151, f32[16,8]{0,1:T(8,128)S(1)} %maximum_maximum_fusion), kind=kOutput, calls=%fused_computation.31 | convolution fusion | flops 50331648 | bytes 3146240 | tf_op jit(solution)/shard_map/ja,cab->cjb/dot_general | solution.py:19
  50.5 0.1 fusion.87
  50.6 0.7 copy.79
  51.3 1.8 %convolution_bitcast_fusion.1 = f32[256,2,8,128]{3,2,1,0:T(8,128)S(1)} fusion(f32[256,8,128]{2,1,0:T(8,128)S(1)} %bitcast.150, f32[16,8]{0,1:T(8,128)S(1)} %maximum_maximum_fusion), kind=kOutput, calls=%fused_computation.30 | convolution fusion | flops 50331648 | bytes 3146240 | tf_op jit(solution)/shard_map/ja,cab->cjb/dot_general | solution.py:19
  53.2 0.0 copy-start
  53.2 0.1 fusion.86
  53.3 1.1 copy-done
  54.4 1.2 %multiply_subtract_fusion.2 = (f32[256,1,8,128]{3,0,1,2:T(8,128)S(1)}, f32[256,1,8,128]{3,0,1,2:T(8,128)S(1)}, f32[256,1,8,128]{3,0,1,2:T(8,128)S(1)}, f32[256,1...) fusion(f32[256,1,8,128]{3,2,1,0:T(8,128)S(1)} %get-tuple-element.19, ...), kind=kLoop, calls=%fused_computation.44 | loop fusion | flops 4718592 | bytes 12591104 | tf_op jit(solution)/shard_map/sub | solution.py:73
  55.6 2.0 %fusion.21 = f32[256,2,8,128]{0,3,2,1:T(8,128)S(1)} fusion(f32[256,1,8,128]{3,0,1,2:T(8,128)S(1)} %get-tuple-element.40, f32[256,1,8,128]{3,0,1,2:T(8,128)S(1)} %get-tuple-element.41, f32[1,128,2,128]{1,3,0,2:T(8,128)S(1)} %get-tuple-element.31, f32[1,128,2,128]{1,3,0,2:T(8,128)S(1)} %get-tuple-element.34), kind=kOutput, calls=%fused_computation.29 | convolution fusion | flops 1611202560 | bytes 4456448 | tf_op jit(solution)/shard_map/cpjb,pbqm->cqjm/dot_general | solution.py:19
  57.5 2.0 %fusion.20 = f32[256,2,8,128]{0,3,2,1:T(8,128)S(1)} fusion(f32[256,1,8,128]{3,0,1,2:T(8,128)S(1)} %get-tuple-element.38, f32[256,1,8,128]{3,0,1,2:T(8,128)S(1)} %get-tuple-element.39, f32[1,128,2,128]{1,3,0,2:T(8,128)S(1)} %get-tuple-element.31, f32[1,128,2,128]{1,3,0,2:T(8,128)S(1)} %get-tuple-element.34), kind=kOutput, calls=%fused_computation.28 | convolution fusion | flops 1611202560 | bytes 4456448 | tf_op jit(solution)/shard_map/cpjb,pbqm->cqjm/dot_general | solution.py:19
  59.5 2.2 %fusion.19 = f32[256,2,8,128]{0,3,2,1:T(8,128)S(1)} fusion(f32[256,1,8,128]{3,0,1,2:T(8,128)S(1)} %get-tuple-element.9, f32[256,1,8,128]{3,0,1,2:T(8,128)S(1)} %get-tuple-element.8, f32[1,128,2,128]{1,3,0,2:T(8,128)S(1)} %get-tuple-element.31, f32[1,128,2,128]{1,3,0,2:T(8,128)S(1)} %get-tuple-element.34), kind=kOutput, calls=%fused_computation.27 | convolution fusion | flops 1611202560 | bytes 4456448 | tf_op jit(solution)/shard_map/cpjb,pbqm->cqjm/dot_general | solution.py:19
  61.7 0.0 copy-start.2
  61.7 0.5 multiply_add_fusion.1
  62.3 0.3 copy-done.2
  62.6 3.6 %fusion.22 = f32[256,2,8,128]{3,0,1,2:T(8,128)S(1)} fusion(f32[256,1,8,128]{0,3,2,1:T(8,128)S(1)} %get-tuple-element.16, f32[256,1,8,128]{0,3,2,1:T(8,128)S(1)} %get-tuple-element.17, f32[1,128,2,128]{1,3,2,0:T(8,128)S(1)} %copy-done.2, f32[1,128,2,128]{1,3,2,0:T(8,128)S(1)} %get-tuple-element.30), kind=kOutput, calls=%fused_computation.32 | convolution fusion | flops 1611202560 | bytes 4456448 | tf_op jit(solution)/shard_map/cqjm,qmpb->cpjb/dot_general | solution.py:19
  66.2 3.6 %fusion.25 = f32[256,2,8,128]{3,0,1,2:T(8,128)S(1)} fusion(f32[256,1,8,128]{0,3,2,1:T(8,128)S(1)} %get-tuple-element.3, f32[256,1,8,128]{0,3,2,1:T(8,128)S(1)} %get-tuple-element.2, f32[1,128,2,128]{1,3,2,0:T(8,128)S(1)} %copy-done.2, f32[1,128,2,128]{1,3,2,0:T(8,128)S(1)} %get-tuple-element.30), kind=kOutput, calls=%fused_computation.33 | convolution fusion | flops 1611202560 | bytes 4456448 | tf_op jit(solution)/shard_map/cqjm,qmpb->cpjb/dot_general | solution.py:19
  69.9 0.6 multiply_add_fusion
  70.5 0.0 copy-start.4
  70.5 0.0 copy-start.5
  70.5 0.2 pad_maximum_fusion.1
  70.7 0.5 copy-done.4
  71.2 0.0 copy-done.5
  71.2 2.4 %fusion.34 = f32[256,4,128]{2,1,0:T(4,128)S(1)} fusion(f32[256,2,8,128]{3,0,1,2:T(8,128)S(1)} %pad_maximum_fusion.1, f32[4,8]{1,0:T(4,128)S(1)} %copy-done.4, f32[4,8]{1,0:T(4,128)S(1)} %copy-done.5), kind=kOutput, calls=%fused_computation.36 | convolution fusion | flops 25296960 | bytes 2621696 | tf_op jit(solution)/shard_map/aj,cjb->cab/dot_general | solution.py:19
  73.6 1.0 all_gather_reshape_reshape.3
  74.6 0.0 all-gather.2.cloned.1.call-update
  74.6 0.0 copy-start.7
  74.6 0.2 pad_maximum_fusion
  74.8 0.5 copy-done.7
  75.3 2.6 %fusion.28 = f32[256,128,8]{1,2,0:T(8,128)S(1)} fusion(f32[256,2,8,128]{3,0,1,2:T(8,128)S(1)} %pad_maximum_fusion, f32[4,8]{1,0:T(4,128)S(1)} %copy-done.5, f32[4,8]{1,0:T(4,128)S(1)} %copy-done.7, f32[4,8]{1,0:T(4,128)S(1)} %copy-done.4), kind=kOutput, calls=%fused_computation.34 | convolution fusion | flops 50594176 | bytes 3146112 | tf_op jit(solution)/shard_map/aj,cjb->cab/dot_general | solution.py:19
  77.9 0.0 copy-start.6
  77.9 0.2 fusion.89
  78.1 0.6 copy.76
  78.7 0.6 copy.77
  79.4 1.9 %fusion.37 = f32[1,256,512]{1,0,2:T(1,128)S(1)} fusion(f32[256,1,4,128]{0,1,3,2:T(1,128)S(1)} %copy.77, f32[256,1,4,128]{0,1,3,2:T(1,128)S(1)} %copy.76, f32[512]{0:T(512)S(1)} %bitcast.160, f32[512]{0:T(512)S(1)} %copy-done.6), kind=kLoop, calls=%fused_computation.56 | loop fusion | flops 393216 | bytes 1576960 | tf_op jit(solution)/shard_map/add | solution.py:120
  81.3 16.4 %all_to_all.45 = f32[1,256,512]{1,0,2:T(1,128)S(1)} all-to-all(f32[1,256,512]{1,0,2:T(1,128)S(1)} %fusion.37), channel_id=1, replica_groups=mesh['seq'=4,'chan'=4,'rep'=2] {'seq'}, dimensions={2} | all-to-all | bytes 1048576 | tf_op jit(solution)/shard_map/all_to_all | solution.py:123
  97.8 1.0 copy.78
  98.8 2.1 %reduce_sum.11 = f32[256,512]{1,0:T(8,128)} reduce(f32[2,1,256,512]{3,2,1,0:T(8,128)} %all-gather.2.cloned.1.call-done, f32[]{:T(128)} %constant.55.clone.1), dimensions={0,1}, to_apply=%region_0.1 | reduce | flops 131072 | bytes 1572868 | tf_op jit(solution)/shard_map/reduce_sum | solution.py:7
  (7 shorter events, 0.0 us)
Async XLA Ops:
  7.2 20.8 %all-to-all-start = ((f32[4,256,128]{2,1,0:T(8,128)}), f32[4,256,128]{2,1,0:T(8,128)S(1)}, u32[]{:S(2)}, u32[]{:S(2)}) async-start(f32[4,256,128]{2,1,0:T(8,128)} %bitcast.153), calls=%async_computation | async-start | bytes 1048576 | tf_op jit(solution)/shard_map/all_to_all | solution.py:152
  13.6 0.6 copy-start.3
  28.0 8.4 %copy-start.1 = (f32[4,256,128]{2,1,0:T(8,128)}, f32[4,256,128]{2,1,0:T(8,128)S(1)}, u32[]{:S(2)}) copy-start(f32[4,256,128]{2,1,0:T(8,128)S(1)} %all-to-all-done) | copy-start | bytes 1572868
  28.0 18.2 %all-to-all-start.2 = ((f32[4,256,128]{2,1,0:T(8,128)}), f32[4,256,128]{2,1,0:T(8,128)}, u32[]{:S(2)}, u32[]{:S(2)}) async-start(f32[4,256,128]{2,1,0:T(8,128)} %bitcast.154), calls=%async_computation.2 | async-start | bytes 1048576 | tf_op jit(solution)/shard_map/all_to_all | solution.py:151
  32.2 66.6 %all-gather.2.cloned.1.call-start = ((), (), s32[]{:S(2)}) async-start(), calls=%async_computation.3 | async-start | bytes 1572864 | tf_op jit(solution)/shard_map/all_gather | solution.py:7
  53.2 1.2 %copy-start = (f32[256,1,8,128]{3,2,1,0:T(8,128)S(1)}, f32[256,1,8,128]{3,2,1,0:T(8,128)}, u32[]{:S(2)}) copy-start(f32[256,1,8,128]{3,2,1,0:T(8,128)} %get-tuple-element.23) | copy-start | bytes 3145732
  61.7 0.9 copy-start.2
  70.5 0.7 copy-start.4
  70.5 0.7 copy-start.5
  74.6 0.7 copy-start.7
  77.9 1.4 %copy-start.6 = (f32[512]{0:T(512)S(1)}, f32[512]{0:T(512)}, u32[]{:S(2)}) copy-start(f32[512]{0:T(512)} %broadcast_subtract_fusion.1) | copy-start | bytes 6148
Sparse Core Ops, SparseCore 0:
  74.7 20.3 all-gather.1
